TPU v7x, 32 devices: a whole 2x2x4 slice. The times are simulated.
32 devices in a mesh: gx: 4 (over z), gy: 4 (over y, x), gz: 2 (over core).
Axes of the slice: x: 2, y: 2, z: 4, core: 2. Of those that a mesh axis runs over, the one named last changes fastest.
Arguments:
- velocity: float32 [3, 64, 64, 256], P(None, 'gx', 'gy', 'gz'), may hold values from -6 to 6
Outputs:
- stress_residual: float32 [6, 2048], P(None, ('gx', 'gy', 'gz'))
- coefficients: float32 [96, 6], replicated
All inputs are finite; a program needn't handle non-finite values.
Results may differ from a plain program's by a relative error of at most 0.0042.
Values may be sent and summed in bfloat16 or wider, within the bound.
No kernel may reach another device: no remote copies, remote signals or barrier semaphores. Data moves between devices by JAX's collectives and lax.ppermute only.
A program may use at most 64 MiB of HBM per device.

v0:
```python
import jax
import jax.numpy as jnp
import numpy as np
from jax import lax
from jax.sharding import PartitionSpec as P

PRECISE = lax.Precision.HIGHEST
INDEX_PAIRS = ((0, 0), (1, 1), (2, 2), (0, 1), (0, 2), (1, 2))
WIDTHS = (3.0, 6.0, 12.0)


def extended(block, sides, width):
    for axis, dim in sides:
        count = lax.axis_size(axis)
        forward = [(i, i + 1) for i in range(count - 1)]
        forward.append((count - 1, 0))
        backward = [(target, source) for source, target in forward]
        low = lax.ppermute(
            lax.slice_in_dim(block, block.shape[dim] - width, None, axis=dim), axis, forward
        )
        high = lax.ppermute(lax.slice_in_dim(block, 0, width, axis=dim), axis, backward)
        block = jnp.concatenate([low, block, high], axis=dim)
    return block


def window_table(combos):
    weights_table = np.zeros((len(combos), 16), np.float32)
    for row_index in range(len(combos)):
        box_width, offset = combos[row_index]
        low_edge = 7.5 + offset - box_width / 2.0
        high_edge = 7.5 + offset + box_width / 2.0
        for cell_index in range(16):
            cell_share = min(cell_index + 0.5, high_edge) - max(cell_index - 0.5, low_edge)
            weights_table[row_index, cell_index] = max(cell_share, 0.0) / box_width
    return weights_table


def velocity_combos():
    return [(box_width, offset) for box_width in WIDTHS for offset in (-2.0, 0.0, 2.0)]


def product_combos():
    return [(3.0, 0.0), (12.0, 0.0)]


def matrix_product(left_matrix, right_matrix):
    return [
        [
            left_matrix[i][0] * right_matrix[0][j]
            + left_matrix[i][1] * right_matrix[1][j]
            + left_matrix[i][2] * right_matrix[2][j]
            for j in range(3)
        ]
        for i in range(3)
    ]


def pick_pairs(matrix):
    return [matrix[i][j] for i, j in INDEX_PAIRS]


def build_rows(box_means, pair_means):
    feature_rows = []
    centre_values = []
    for width_index in range(3):
        middle = 3 * width_index + 1
        scaled = WIDTHS[width_index] ** 2 * 0.25

        def offset_value(component, direction, step_size):
            position_list = [middle, middle, middle]
            position_list[direction] = middle + step_size
            return box_means[component, position_list[0], position_list[1], position_list[2]]

        centre_values.append([box_means[i, middle, middle, middle] for i in range(3)])
        gradient = [
            [(offset_value(i, j, 1) - offset_value(i, j, -1)) * scaled for j in range(3)]
            for i in range(3)
        ]
        strain = [[(gradient[i][j] + gradient[j][i]) * 0.5 for j in range(3)] for i in range(3)]
        spin_part = [[(gradient[i][j] - gradient[j][i]) * 0.5 for j in range(3)] for i in range(3)]
        square_strain = matrix_product(strain, strain)
        first_order = matrix_product(strain, spin_part)
        second_order = matrix_product(spin_part, strain)
        commutator = [[first_order[i][j] - second_order[i][j] for j in range(3)] for i in range(3)]
        spin_square = matrix_product(spin_part, spin_part)
        magnitude = sum((strain[i][j] * strain[i][j] for i in range(3) for j in range(3)))
        feature_rows += (
            pick_pairs(strain)
            + pick_pairs(square_strain)
            + pick_pairs(commutator)
            + pick_pairs(spin_square)
        )
        feature_rows += [magnitude * entry for entry in pick_pairs(strain)]
    small_box = centre_values[0]
    large_box = centre_values[2]
    feature_rows += [
        pair_means[index, 0] - small_box[i] * small_box[j]
        for index, (i, j) in enumerate(INDEX_PAIRS)
    ]
    target_rows = [
        pair_means[index, 1] - large_box[i] * large_box[j]
        for index, (i, j) in enumerate(INDEX_PAIRS)
    ]
    return (jnp.stack(feature_rows), jnp.stack(target_rows))


def solve_fit(gram_matrix, sample_total):
    scales = jnp.sqrt(jnp.diagonal(gram_matrix) / sample_total + 1e-06)
    feature_scale = scales[:96]
    normal = gram_matrix[:96, :96] / (
        sample_total * feature_scale[:, None] * feature_scale[None, :]
    ) + 0.1 * jnp.eye(96, dtype=jnp.float32)
    target_side = gram_matrix[:96, 96:] / (sample_total * feature_scale[:, None])
    factor = jnp.linalg.cholesky(normal)
    solved = jax.scipy.linalg.cho_solve((factor, True), target_side)
    return (solved / feature_scale[:, None], scales[96:])


def axis_weights(length, weights_table):
    sample_count = length // 8
    combo_count = weights_table.shape[0]
    full_table = np.zeros((sample_count * combo_count, length + 8), np.float32)
    for sample_index in range(sample_count):
        full_table[
            sample_index * combo_count : (sample_index + 1) * combo_count,
            8 * sample_index : 8 * sample_index + 16,
        ] = weights_table
    return jnp.asarray(full_table)


def windowed(wide_field, weights_table):
    along_z = jnp.einsum(
        "cxyz,kz->cxyk",
        wide_field,
        axis_weights(wide_field.shape[3] - 8, weights_table),
        precision=PRECISE,
    )
    along_y = jnp.einsum(
        "cxyk,jy->cxjk",
        along_z,
        axis_weights(wide_field.shape[2] - 8, weights_table),
        precision=PRECISE,
    )
    return jnp.einsum(
        "cxjk,ix->cijk",
        along_y,
        axis_weights(wide_field.shape[1] - 8, weights_table),
        precision=PRECISE,
    )


def shards(velocity):
    rounded = velocity.astype(jnp.bfloat16)
    padded = extended(rounded, (("gx", 1), ("gy", 2), ("gz", 3)), 4)
    wide_field = padded.astype(jnp.float32)
    count_x = velocity.shape[1] // 8
    count_y = velocity.shape[2] // 8
    count_z = velocity.shape[3] // 8
    samples = count_x * count_y * count_z
    box_means = windowed(wide_field, window_table(velocity_combos()))
    box_means = box_means.reshape(3, count_x, 9, count_y, 9, count_z, 9)
    box_means = jnp.transpose(box_means, (0, 2, 4, 6, 1, 3, 5)).reshape(3, 9, 9, 9, samples)
    pair_field = jnp.stack([wide_field[i] * wide_field[j] for i, j in INDEX_PAIRS])
    pair_means = windowed(pair_field, window_table(product_combos())).reshape(
        6, count_x, 2, count_y, 2, count_z, 2
    )
    pair_means = jnp.stack(
        [pair_means[:, :, 0, :, 0, :, 0], pair_means[:, :, 1, :, 1, :, 1]], axis=1
    )
    pair_means = pair_means.reshape(6, 2, samples)
    features, targets = build_rows(box_means, pair_means)
    stacked = jnp.concatenate([features, targets], axis=0)
    local_gram = jnp.dot(stacked, stacked.T, precision=PRECISE, preferred_element_type=jnp.float32)
    gram_matrix = lax.psum(local_gram, ("gx", "gy", "gz"))
    sample_total = float(samples * lax.axis_size("gx") * lax.axis_size("gy") * lax.axis_size("gz"))
    coefficients, target_scale = solve_fit(gram_matrix, sample_total)
    predicted = jnp.dot(
        coefficients.T, features, precision=PRECISE, preferred_element_type=jnp.float32
    )
    residual = (targets - predicted) / target_scale[:, None]
    return (residual, coefficients)


def solution(mesh):
    in_specs = (P(None, "gx", "gy", "gz"),)
    out_specs = (P(None, ("gx", "gy", "gz")), P())
    return jax.shard_map(shards, mesh=mesh, in_specs=in_specs, out_specs=out_specs, check_vma=False)
```

profile of v0, /device:TPU:0, one launch (start us, length us, event | category | flops | bytes accessed | tf_op | source)
XLA Modules:
  0.0 118.4 jit_solution(10109509089073360371)
XLA Ops:
  0.6 1.0 convert_element_type.7
  1.7 0.0 copy-start.8
  1.7 3.1 %collective-permute-start = (bf16[3,4,16,128]{3,2,1,0:T(8,128)(2,1)S(1)}, bf16[3,4,16,128]{3,2,1,0:T(8,128)(2,1)S(1)}, u32[]{:S(2)}, u32[]{:S(2)}) collective-permute-start(bf16[3,4,16,128]{3,2,1,0:T(8,128)(2,1)S(1)} %get-tuple-element.102), channel_id=1, source_target_pairs={{0,8},{8,16},{16,24},{24,0},{1,9},{9,17},{17,25},{25,1},{2,10},{10... | collective-permute-start | bytes 147464 | tf_op jit(solution)/shard_map/ppermute | solution.py:18
  4.8 2.1 %collective-permute-start.1 = (bf16[3,4,16,128]{3,2,1,0:T(8,128)(2,1)S(1)}, bf16[3,4,16,128]{3,2,1,0:T(8,128)(2,1)S(1)}, u32[]{:S(2)}, u32[]{:S(2)}) collective-permute-start(bf16[3,4,16,128]{3,2,1,0:T(8,128)(2,1)S(1)} %get-tuple-element.103), channel_id=1, source_target_pairs={{8,0},{16,8},{24,16},{0,24},{9,1},{17,9},{25,17},{1,25},{10,2},{18... | collective-permute-start | bytes 147464 | tf_op jit(solution)/shard_map/ppermute | solution.py:21
  6.9 2.1 %collective-permute-done = bf16[3,4,16,128]{3,2,1,0:T(8,128)(2,1)S(1)} collective-permute-done((bf16[3,4,16,128]{3,2,1,0:T(8,128)(2,1)S(1)}, bf16[3,4,16,128]{3,2,1,0:T(8,128)(2,1)S(1)}, u32[]{:S(2)}, u32[]{:S(2)}) %collective-permute-start) | collective-permute-done | bytes 49184 | tf_op jit(solution)/shard_map/ppermute | solution.py:18
  9.0 0.4 collective-permute-done.1
  9.4 0.1 pad_maximum_fusion.4
  9.5 1.5 %collective-permute-start.2 = (bf16[3,24,4,128]{3,2,1,0:T(4,128)(2,1)S(1)}, bf16[3,24,4,128]{3,2,1,0:T(4,128)(2,1)S(1)}, u32[]{:S(2)}, u32[]{:S(2)}) collective-permute-start(bf16[3,24,4,128]{3,2,1,0:T(4,128)(2,1)S(1)} %get-tuple-element.100), channel_id=1, source_target_pairs={{0,2},{2,4},{4,6},{6,0},{1,3},{3,5},{5,7},{7,1},{8,10},{10,12},{12... | collective-permute-start | bytes 221192 | tf_op jit(solution)/shard_map/ppermute | solution.py:18
  11.0 1.4 %collective-permute-start.3 = (bf16[3,24,4,128]{3,2,1,0:T(4,128)(2,1)S(1)}, bf16[3,24,4,128]{3,2,1,0:T(4,128)(2,1)S(1)}, u32[]{:S(2)}, u32[]{:S(2)}) collective-permute-start(bf16[3,24,4,128]{3,2,1,0:T(4,128)(2,1)S(1)} %get-tuple-element.101), channel_id=1, source_target_pairs={{2,0},{4,2},{6,4},{0,6},{3,1},{5,3},{7,5},{1,7},{10,8},{12,10},{14... | collective-permute-start | bytes 221192 | tf_op jit(solution)/shard_map/ppermute | solution.py:21
  12.5 2.3 %collective-permute-done.2 = bf16[3,24,4,128]{3,2,1,0:T(4,128)(2,1)S(1)} collective-permute-done((bf16[3,24,4,128]{3,2,1,0:T(4,128)(2,1)S(1)}, bf16[3,24,4,128]{3,2,1,0:T(4,128)(2,1)S(1)}, u32[]{:S(2)}, u32[]{:S(2)}) %collective-permute-start.2) | collective-permute-done | bytes 73760 | tf_op jit(solution)/shard_map/ppermute | solution.py:18
  14.8 0.8 collective-permute-done.3
  15.6 0.2 pad_maximum_fusion.1
  15.9 0.2 fusion.156
  16.1 0.1 collective-permute-start.4
  16.2 0.5 collective-permute-start.5
  16.7 1.3 %collective-permute-done.4 = bf16[3,24,24,4]{3,2,1,0:T(8,128)(2,1)S(1)} collective-permute-done((bf16[3,24,24,4]{3,2,1,0:T(8,128)(2,1)S(1)}, bf16[3,24,24,4]{3,2,1,0:T(8,128)(2,1)S(1)}, u32[]{:S(2)}, u32[]{:S(2)}) %collective-permute-start.4) | collective-permute-done | bytes 13856 | tf_op jit(solution)/shard_map/ppermute | solution.py:18
  17.9 0.6 collective-permute-done.5
  18.6 0.0 copy-done.8
  18.6 1.3 %fusion.124 = f32[3,24,24,144]{3,2,1,0:T(8,128)S(1)} fusion(f32[144,136,1,1]{0,1,3,2:T(8,128)S(1)} %copy-done.8, bf16[3,24,24,4]{3,2,1,0:T(8,128)(2,1)S(1)} %collective-permute-done.5, bf16[3,24,4,128]{3,2,1,0:T(4,128)(2,1)S(1)} %collective-permute-done.3, bf16[3,4,16,128]{3,2,1,0:T(8,128)(2,1)S(1)} %collective-permute-done.1, ...), kind=kOutput, calls=%fused_computation.402 | convolution fusion | flops 409383936 | bytes 1543680 | tf_op jit(solution)/shard_map/cxyz,kz->cxyk/dot_general | solution.py:132
  19.9 1.6 %convolution_bitcast_fusion = f32[3,24,18,144]{3,2,1,0:T(8,128)S(1)} fusion(f32[3,24,24,144]{3,2,1,0:T(8,128)S(1)} %fusion.124, f32[18,24,1,1]{1,0,3,2:T(8,128)S(1)} %copy-done.4), kind=kOutput, calls=%fused_computation.1 | convolution fusion | flops 53747712 | bytes 1743552 | tf_op jit(solution)/shard_map/cxyk,jy->cxjk/dot_general | solution.py:138
  21.5 1.6 %convolution_bitcast_fusion.1 = f32[3,18,18,144]{3,1,2,0:T(8,128)S(1)} fusion(f32[18,24,1,1]{1,0,3,2:T(8,128)S(1)} %copy-done.4, f32[3,24,18,144]{3,2,1,0:T(8,128)S(1)} %convolution_bitcast_fusion), kind=kOutput, calls=%fused_computation.2 | convolution fusion | flops 40310784 | bytes 1308096 | tf_op jit(solution)/shard_map/cxjk,ix->cijk/dot_general | solution.py:144
  23.1 0.3 copy.30
  23.5 6.3 %reshape.6592 = f32[3,2,9,2,9,16,9]{6,5,4,3,2,1,0:T(8,128)} reshape(f32[3,18,18,144]{3,2,1,0:T(8,128)S(1)} %copy.30) | data formatting | bytes 1119744 | tf_op jit(solution)/shard_map/reshape | solution.py:161
  29.8 11.0 %copy.31 = f32[3,9,9,9,2,2,16]{6,5,4,0,3,2,1:T(2,128)} copy(f32[3,9,9,9,2,2,16]{3,6,2,5,1,4,0:T(8,128)} %bitcast.897) | data formatting | bytes 1119744 | tf_op jit(solution)/shard_map/transpose | solution.py:162
  40.8 5.8 %reshape.6593 = f32[3,9,9,9,64]{4,0,3,2,1:T(4,128)S(1)} reshape(f32[3,9,9,9,2,2,16]{6,5,4,0,3,2,1:T(2,128)} %copy.31) | data formatting | bytes 1119744 | tf_op jit(solution)/shard_map/reshape | solution.py:162
  46.7 0.8 fusion.125
  47.6 0.1 multiply_dynamic-update-slice_fusion.2
  47.7 0.0 copy-start.5
  47.7 0.1 multiply_dynamic-update-slice_fusion.1
  47.8 0.1 multiply_dynamic-update-slice_fusion
  47.9 0.6 copy-done.5
  48.5 2.9 %fusion.158 = f32[6,24,24,32]{3,2,1,0:T(8,128)S(1)} fusion(f32[6,24,24,136]{3,2,1,0:T(8,128)S(1)} %multiply_dynamic-update-slice_fusion, f32[32,136,1,1]{1,0,3,2:T(8,128)S(1)} %copy-done.5), kind=kOutput, calls=%fused_computation.409 | convolution fusion | flops 180486144 | bytes 2339840 | tf_op jit(solution)/shard_map/cxyz,kz->cxyk/dot_general | solution.py:132
  51.4 1.0 convolution_bitcast_fusion.2
  52.5 0.3 convolution_bitcast_fusion.3
  52.8 0.2 copy.28
  52.9 2.0 %slice_reduce_fusion = (f32[2,2,16]{2,1,0:T(2,128)S(1)}, f32[2,2,16]{2,1,0:T(2,128)S(1)}, f32[2,2,16]{2,1,0:T(2,128)S(1)}, f32[2,2,16]{2,1,0:T(2,128)S(1)}, f32[...) fusion(f32[6,2,2,2,2,16,2]{0,6,5,4,3,2,1:T(2,128)S(1)} %bitcast.898), kind=kLoop, calls=%fused_computation.34 | loop fusion | bytes 6144 | tf_op jit(solution)/shard_map/slice | solution.py:97
  55.0 0.1 squeeze.35
  55.1 0.1 squeeze.34
  55.1 0.1 squeeze.33
  55.2 0.1 squeeze.32
  55.3 0.1 squeeze.31
  55.4 0.1 squeeze.30
  55.5 0.1 squeeze.29
  55.6 0.1 squeeze.28
  55.6 0.1 squeeze.27
  55.7 0.1 squeeze.26
  55.8 0.1 squeeze.25
  55.9 0.1 squeeze.24
  56.4 0.3 stack.8
  56.7 0.3 concatenate.21
  57.0 0.2 fusion.159
  57.3 40.3 %psum.7 = f32[102,102]{1,0:T(8,128)S(1)} all-reduce(f32[102,102]{1,0:T(8,128)S(1)} %fusion.159), channel_id=1, replica_groups=mesh['gx'=4,'gy'=4,'gz'=2] {'gx','gy','gz'}, use_global_device_ids=true, to_apply=%region_0.0 | all-reduce | flops 10404 | bytes 83232 | tf_op jit(solution)/shard_map/psum | solution.py:174
  97.6 1.7 %gather_fusion = f32[102]{0:T(128)S(1)} fusion(f32[102,102]{1,0:T(8,128)S(1)} %psum.7, s32[102]{0:T(128)S(1)} %or_bitcast_fusion), kind=kCustom, calls=%fused_computation | custom fusion | bytes 1632 | tf_op jit(solution)/shard_map/jit(diagonal)/cond/branch_0_fun/gather | solution.py:108
  99.3 0.1 slice.404
  99.3 0.1 fusion.5
  99.4 0.1 copy.32
  99.5 0.1 fusion.8
  99.6 8.8 %cholesky.16 = f32[96,96]{1,0:T(8,128)S(1)} custom-call(f32[96,96]{1,0:T(8,128)S(1)} %fusion.8), custom_call_target="Cholesky" | custom-call | tf_op jit(solution)/shard_map/jit(cholesky)/cholesky | solution.py:114
  108.4 0.6 compare_reduce_fusion
  109.1 0.7 fusion.3
  109.7 7.4 %custom-call.10 = f32[1,96,96]{1,2,0:T(8,128)S(1)} custom-call(f32[1,96,96]{2,1,0:T(8,128)S(1)} %fusion.3), custom_call_target="InvertDiagBlocksLowerTriangular" | custom-call | tf_op jit(solution)/shard_map/jit(_cho_solve)/triangular_solve | solution.py:115
  117.1 0.3 fusion.4
  117.4 0.2 convolution_divide_fusion
  117.6 0.8 fusion.1
  (46 shorter events, 0.6 us)
Async XLA Ops:
  1.7 16.9 %copy-start.8 = (f32[144,136,1,1]{0,1,3,2:T(8,128)S(1)}, f32[144,136,1,1]{0,1,3,2:T(8,128)}, u32[]{:S(2)}) copy-start(f32[144,136,1,1]{0,1,3,2:T(8,128)} %constant.98) | copy-start | bytes 235012
  1.7 7.3 %collective-permute-start = (bf16[3,4,16,128]{3,2,1,0:T(8,128)(2,1)S(1)}, bf16[3,4,16,128]{3,2,1,0:T(8,128)(2,1)S(1)}, u32[]{:S(2)}, u32[]{:S(2)}) collective-permute-start(bf16[3,4,16,128]{3,2,1,0:T(8,128)(2,1)S(1)} %get-tuple-element.102), channel_id=1, source_target_pairs={{0,8},{8,16},{16,24},{24,0},{1,9},{9,17},{17,25},{25,1},{2,10},{10... | collective-permute-start | bytes 147464 | tf_op jit(solution)/shard_map/ppermute | solution.py:18
  4.8 4.6 %collective-permute-start.1 = (bf16[3,4,16,128]{3,2,1,0:T(8,128)(2,1)S(1)}, bf16[3,4,16,128]{3,2,1,0:T(8,128)(2,1)S(1)}, u32[]{:S(2)}, u32[]{:S(2)}) collective-permute-start(bf16[3,4,16,128]{3,2,1,0:T(8,128)(2,1)S(1)} %get-tuple-element.103), channel_id=1, source_target_pairs={{8,0},{16,8},{24,16},{0,24},{9,1},{17,9},{25,17},{1,25},{10,2},{18... | collective-permute-start | bytes 147464 | tf_op jit(solution)/shard_map/ppermute | solution.py:21
  9.4 10.5 %copy-start.2 = (bf16[3,4,16,128]{3,2,1,0:T(8,128)(2,1)}, bf16[3,4,16,128]{3,2,1,0:T(8,128)(2,1)S(1)}, u32[]{:S(2)}) copy-start(bf16[3,4,16,128]{3,2,1,0:T(8,128)(2,1)S(1)} %collective-permute-done.1) | copy-start | bytes 147460
  9.5 5.3 %collective-permute-start.2 = (bf16[3,24,4,128]{3,2,1,0:T(4,128)(2,1)S(1)}, bf16[3,24,4,128]{3,2,1,0:T(4,128)(2,1)S(1)}, u32[]{:S(2)}, u32[]{:S(2)}) collective-permute-start(bf16[3,24,4,128]{3,2,1,0:T(4,128)(2,1)S(1)} %get-tuple-element.100), channel_id=1, source_target_pairs={{0,2},{2,4},{4,6},{6,0},{1,3},{3,5},{5,7},{7,1},{8,10},{10,12},{12... | collective-permute-start | bytes 221192 | tf_op jit(solution)/shard_map/ppermute | solution.py:18
  11.0 4.6 %collective-permute-start.3 = (bf16[3,24,4,128]{3,2,1,0:T(4,128)(2,1)S(1)}, bf16[3,24,4,128]{3,2,1,0:T(4,128)(2,1)S(1)}, u32[]{:S(2)}, u32[]{:S(2)}) collective-permute-start(bf16[3,24,4,128]{3,2,1,0:T(4,128)(2,1)S(1)} %get-tuple-element.101), channel_id=1, source_target_pairs={{2,0},{4,2},{6,4},{0,6},{3,1},{5,3},{7,5},{1,7},{10,8},{12,10},{14... | collective-permute-start | bytes 221192 | tf_op jit(solution)/shard_map/ppermute | solution.py:21
  16.1 1.9 %collective-permute-start.4 = (bf16[3,24,24,4]{3,2,1,0:T(8,128)(2,1)S(1)}, bf16[3,24,24,4]{3,2,1,0:T(8,128)(2,1)S(1)}, u32[]{:S(2)}, u32[]{:S(2)}) collective-permute-start(bf16[3,24,24,4]{3,2,1,0:T(8,128)(2,1)S(1)} %get-tuple-element.98), channel_id=1, source_target_pairs={{0,1},{1,0},{2,3},{3,2},{4,5},{5,4},{6,7},{7,6},{8,9},{9,8},{10,11... | collective-permute-start | bytes 41480 | tf_op jit(solution)/shard_map/ppermute | solution.py:18
  16.2 2.4 %collective-permute-start.5 = (bf16[3,24,24,4]{3,2,1,0:T(8,128)(2,1)S(1)}, bf16[3,24,24,4]{3,2,1,0:T(8,128)(2,1)S(1)}, u32[]{:S(2)}, u32[]{:S(2)}) collective-permute-start(bf16[3,24,24,4]{3,2,1,0:T(8,128)(2,1)S(1)} %get-tuple-element.99), channel_id=1, source_target_pairs={{1,0},{0,1},{3,2},{2,3},{5,4},{4,5},{7,6},{6,7},{9,8},{8,9},{11,10... | collective-permute-start | bytes 41480 | tf_op jit(solution)/shard_map/ppermute | solution.py:21
  16.7 3.3 %copy-start.4 = (f32[18,24,1,1]{1,0,3,2:T(8,128)S(1)}, f32[18,24,1,1]{1,0,3,2:T(8,128)}, u32[]{:S(2)}) copy-start(f32[18,24,1,1]{1,0,3,2:T(8,128)} %constant.99) | copy-start | bytes 5188
  18.6 1.3 %copy-start = (bf16[3,24,24,4]{3,2,1,0:T(8,128)(2,1)}, bf16[3,24,24,4]{3,2,1,0:T(8,128)(2,1)S(1)}, u32[]{:S(2)}) copy-start(bf16[3,24,24,4]{3,2,1,0:T(8,128)(2,1)S(1)} %collective-permute-done.5) | copy-start | bytes 41476
  40.8 5.9 %copy-start.1 = (bf16[3,24,24,4]{3,2,1,0:T(8,128)(2,1)S(1)}, bf16[3,24,24,4]{3,2,1,0:T(8,128)(2,1)}, u32[]{:S(2)}) copy-start(bf16[3,24,24,4]{3,2,1,0:T(8,128)(2,1)} %copy-done) | copy-start | bytes 41476
  40.8 5.9 %copy-start.3 = (bf16[3,4,16,128]{3,2,1,0:T(8,128)(2,1)S(1)}, bf16[3,4,16,128]{3,2,1,0:T(8,128)(2,1)}, u32[]{:S(2)}) copy-start(bf16[3,4,16,128]{3,2,1,0:T(8,128)(2,1)} %copy-done.2) | copy-start | bytes 147460
  47.7 0.8 copy-start.5
  48.5 2.9 %copy-start.6 = (f32[4,24,1,1]{1,0,3,2:T(4,128)S(1)}, f32[4,24,1,1]{1,0,3,2:T(4,128)}, u32[]{:S(2)}) copy-start(f32[4,24,1,1]{1,0,3,2:T(4,128)} %constant.97) | copy-start | bytes 1156
  117.6 0.8 copy-start.7
where the time goes:
time: 119 us; the launch traced here: 118 us
  blocking collectives  40.3 us (34%)
  local copies, waits for them, and re-layouts  29.8 us (25%)
  other arithmetic  20.6 us (17%)
  matrix products  10.3 us (9%)
  starting transfers between devices  8.74 us (7%)
  waiting for transfers between devices  7.6 us (6%)
    psum x1, blocking collectives, shards(): gram_matrix = lax.psum(local_gram, ('gx', 'gy', 'gz'))  40.3 us
    transpose x1, local copies, waits for them, and re-layouts, shards(): jnp.transpose(box_means, (0, 2, 4, 6, 1, 3, 5)).reshape(3, 9, 9, 9, samples)  11 us
    another operation x3, other arithmetic, solve_fit(): factor = jnp.linalg.cholesky(normal)  9.45 us
    another operation x2, other arithmetic, solve_fit(): solved = jax.scipy.linalg.cho_solve((factor, True), target_side)  8.01 us
    reshape x1, local copies, waits for them, and re-layouts, shards(): box_means = box_means.reshape(3, count_x, 9, count_y, 9, count_z, 9)  6.35 us
    reshape x1, local copies, waits for them, and re-layouts, shards(): jnp.transpose(box_means, (0, 2, 4, 6, 1, 3, 5)).reshape(3, 9, 9, 9, samples)  5.76 us
    ppermute x3, waiting for transfers between devices, extended(): lax.ppermute(lax.slice_in_dim(block, block.shape[dim] - width, None, axis...  5.7 us
    ppermute x3, starting transfers between devices, extended(): lax.ppermute(lax.slice_in_dim(block, block.shape[dim] - width, None, axis...  4.72 us
  transfers between devices with their start and end apart: 6, of which 6 were waited for; matrix products, arithmetic and copies ran while one was open for 0% of the time, Pallas kernels for 0%

commit v1 on v0

--- a/solution.py
+++ b/solution.py
@@ -171,7 +171,7 @@
     features, targets = build_rows(box_means, pair_means)
     stacked = jnp.concatenate([features, targets], axis=0)
     local_gram = jnp.dot(stacked, stacked.T, precision=PRECISE, preferred_element_type=jnp.float32)
-    gram_matrix = lax.psum(local_gram, ("gx", "gy", "gz"))
+    gram_matrix = lax.psum(lax.psum(local_gram, ("gy", "gz")), "gx")
     sample_total = float(samples * lax.axis_size("gx") * lax.axis_size("gy") * lax.axis_size("gz"))
     coefficients, target_scale = solve_fit(gram_matrix, sample_total)
     predicted = jnp.dot(

time: 119 us -> 123 us (1.034)
  blocking collectives: 40.3 us -> 44.1 us
    psum x1 -> x2, blocking collectives: 40.3 us -> 44.1 us  [shards(): gram_matrix = lax.psum(lax.psum(local_gram, ('gy', 'gz')), 'gx')]
where the time goes in v1:
time: 123 us; the launch traced here: 122 us
  blocking collectives  44.1 us (36%)
  local copies, waits for them, and re-layouts  29.8 us (24%)
  other arithmetic  20.6 us (17%)
  matrix products  10.3 us (8%)
  starting transfers between devices  8.74 us (7%)
  waiting for transfers between devices  7.6 us (6%)
    psum x2, blocking collectives, shards(): gram_matrix = lax.psum(lax.psum(local_gram, ('gy', 'gz')), 'gx')  44.1 us
    transpose x1, local copies, waits for them, and re-layouts, shards(): jnp.transpose(box_means, (0, 2, 4, 6, 1, 3, 5)).reshape(3, 9, 9, 9, samples)  11 us
    another operation x3, other arithmetic, solve_fit(): factor = jnp.linalg.cholesky(normal)  9.45 us
    another operation x2, other arithmetic, solve_fit(): solved = jax.scipy.linalg.cho_solve((factor, True), target_side)  8.01 us
    reshape x1, local copies, waits for them, and re-layouts, shards(): box_means = box_means.reshape(3, count_x, 9, count_y, 9, count_z, 9)  6.35 us
    reshape x1, local copies, waits for them, and re-layouts, shards(): jnp.transpose(box_means, (0, 2, 4, 6, 1, 3, 5)).reshape(3, 9, 9, 9, samples)  5.76 us
    ppermute x3, waiting for transfers between devices, extended(): lax.ppermute(lax.slice_in_dim(block, block.shape[dim] - width, None, axis...  5.7 us
    ppermute x3, starting transfers between devices, extended(): lax.ppermute(lax.slice_in_dim(block, block.shape[dim] - width, None, axis...  4.72 us
  transfers between devices with their start and end apart: 6, of which 6 were waited for; matrix products, arithmetic and copies ran while one was open for 0% of the time, Pallas kernels for 0%

profile of v1, /device:TPU:0, one launch (start us, length us, event | category | flops | bytes accessed | tf_op | source)
XLA Modules:
  0.0 122.2 jit_solution(15691184890532090186)
XLA Ops:
  0.6 1.0 convert_element_type.7
  1.7 0.0 copy-start.8
  1.7 3.1 %collective-permute-start = (bf16[3,4,16,128]{3,2,1,0:T(8,128)(2,1)S(1)}, bf16[3,4,16,128]{3,2,1,0:T(8,128)(2,1)S(1)}, u32[]{:S(2)}, u32[]{:S(2)}) collective-permute-start(bf16[3,4,16,128]{3,2,1,0:T(8,128)(2,1)S(1)} %get-tuple-element.102), channel_id=1, source_target_pairs={{0,8},{8,16},{16,24},{24,0},{1,9},{9,17},{17,25},{25,1},{2,10},{10... | collective-permute-start | bytes 147464 | tf_op jit(solution)/shard_map/ppermute | solution.py:18
  4.8 2.1 %collective-permute-start.1 = (bf16[3,4,16,128]{3,2,1,0:T(8,128)(2,1)S(1)}, bf16[3,4,16,128]{3,2,1,0:T(8,128)(2,1)S(1)}, u32[]{:S(2)}, u32[]{:S(2)}) collective-permute-start(bf16[3,4,16,128]{3,2,1,0:T(8,128)(2,1)S(1)} %get-tuple-element.103), channel_id=1, source_target_pairs={{8,0},{16,8},{24,16},{0,24},{9,1},{17,9},{25,17},{1,25},{10,2},{18... | collective-permute-start | bytes 147464 | tf_op jit(solution)/shard_map/ppermute | solution.py:21
  6.9 2.1 %collective-permute-done = bf16[3,4,16,128]{3,2,1,0:T(8,128)(2,1)S(1)} collective-permute-done((bf16[3,4,16,128]{3,2,1,0:T(8,128)(2,1)S(1)}, bf16[3,4,16,128]{3,2,1,0:T(8,128)(2,1)S(1)}, u32[]{:S(2)}, u32[]{:S(2)}) %collective-permute-start) | collective-permute-done | bytes 49184 | tf_op jit(solution)/shard_map/ppermute | solution.py:18
  9.0 0.4 collective-permute-done.1
  9.4 0.1 pad_maximum_fusion.4
  9.5 1.5 %collective-permute-start.2 = (bf16[3,24,4,128]{3,2,1,0:T(4,128)(2,1)S(1)}, bf16[3,24,4,128]{3,2,1,0:T(4,128)(2,1)S(1)}, u32[]{:S(2)}, u32[]{:S(2)}) collective-permute-start(bf16[3,24,4,128]{3,2,1,0:T(4,128)(2,1)S(1)} %get-tuple-element.100), channel_id=1, source_target_pairs={{0,2},{2,4},{4,6},{6,0},{1,3},{3,5},{5,7},{7,1},{8,10},{10,12},{12... | collective-permute-start | bytes 221192 | tf_op jit(solution)/shard_map/ppermute | solution.py:18
  11.0 1.4 %collective-permute-start.3 = (bf16[3,24,4,128]{3,2,1,0:T(4,128)(2,1)S(1)}, bf16[3,24,4,128]{3,2,1,0:T(4,128)(2,1)S(1)}, u32[]{:S(2)}, u32[]{:S(2)}) collective-permute-start(bf16[3,24,4,128]{3,2,1,0:T(4,128)(2,1)S(1)} %get-tuple-element.101), channel_id=1, source_target_pairs={{2,0},{4,2},{6,4},{0,6},{3,1},{5,3},{7,5},{1,7},{10,8},{12,10},{14... | collective-permute-start | bytes 221192 | tf_op jit(solution)/shard_map/ppermute | solution.py:21
  12.5 2.3 %collective-permute-done.2 = bf16[3,24,4,128]{3,2,1,0:T(4,128)(2,1)S(1)} collective-permute-done((bf16[3,24,4,128]{3,2,1,0:T(4,128)(2,1)S(1)}, bf16[3,24,4,128]{3,2,1,0:T(4,128)(2,1)S(1)}, u32[]{:S(2)}, u32[]{:S(2)}) %collective-permute-start.2) | collective-permute-done | bytes 73760 | tf_op jit(solution)/shard_map/ppermute | solution.py:18
  14.8 0.8 collective-permute-done.3
  15.6 0.2 pad_maximum_fusion.1
  15.9 0.2 fusion.156
  16.1 0.1 collective-permute-start.4
  16.2 0.5 collective-permute-start.5
  16.7 1.3 %collective-permute-done.4 = bf16[3,24,24,4]{3,2,1,0:T(8,128)(2,1)S(1)} collective-permute-done((bf16[3,24,24,4]{3,2,1,0:T(8,128)(2,1)S(1)}, bf16[3,24,24,4]{3,2,1,0:T(8,128)(2,1)S(1)}, u32[]{:S(2)}, u32[]{:S(2)}) %collective-permute-start.4) | collective-permute-done | bytes 13856 | tf_op jit(solution)/shard_map/ppermute | solution.py:18
  17.9 0.6 collective-permute-done.5
  18.6 1.3 %fusion.124 = f32[3,24,24,144]{3,2,1,0:T(8,128)S(1)} fusion(f32[144,136,1,1]{0,1,3,2:T(8,128)S(1)} %copy-done.8, bf16[3,24,24,4]{3,2,1,0:T(8,128)(2,1)S(1)} %collective-permute-done.5, bf16[3,24,4,128]{3,2,1,0:T(4,128)(2,1)S(1)} %collective-permute-done.3, bf16[3,4,16,128]{3,2,1,0:T(8,128)(2,1)S(1)} %collective-permute-done.1, ...), kind=kOutput, calls=%fused_computation.402 | convolution fusion | flops 409383936 | bytes 1543680 | tf_op jit(solution)/shard_map/cxyz,kz->cxyk/dot_general | solution.py:132
  19.9 1.6 %convolution_bitcast_fusion = f32[3,24,18,144]{3,2,1,0:T(8,128)S(1)} fusion(f32[3,24,24,144]{3,2,1,0:T(8,128)S(1)} %fusion.124, f32[18,24,1,1]{1,0,3,2:T(8,128)S(1)} %copy-done.4), kind=kOutput, calls=%fused_computation.1 | convolution fusion | flops 53747712 | bytes 1743552 | tf_op jit(solution)/shard_map/cxyk,jy->cxjk/dot_general | solution.py:138
  21.5 1.6 %convolution_bitcast_fusion.1 = f32[3,18,18,144]{3,1,2,0:T(8,128)S(1)} fusion(f32[18,24,1,1]{1,0,3,2:T(8,128)S(1)} %copy-done.4, f32[3,24,18,144]{3,2,1,0:T(8,128)S(1)} %convolution_bitcast_fusion), kind=kOutput, calls=%fused_computation.2 | convolution fusion | flops 40310784 | bytes 1308096 | tf_op jit(solution)/shard_map/cxjk,ix->cijk/dot_general | solution.py:144
  23.1 0.3 copy.30
  23.5 6.3 %reshape.6592 = f32[3,2,9,2,9,16,9]{6,5,4,3,2,1,0:T(8,128)} reshape(f32[3,18,18,144]{3,2,1,0:T(8,128)S(1)} %copy.30) | data formatting | bytes 1119744 | tf_op jit(solution)/shard_map/reshape | solution.py:161
  29.8 11.0 %copy.31 = f32[3,9,9,9,2,2,16]{6,5,4,0,3,2,1:T(2,128)} copy(f32[3,9,9,9,2,2,16]{3,6,2,5,1,4,0:T(8,128)} %bitcast.897) | data formatting | bytes 1119744 | tf_op jit(solution)/shard_map/transpose | solution.py:162
  40.8 5.8 %reshape.6593 = f32[3,9,9,9,64]{4,0,3,2,1:T(4,128)S(1)} reshape(f32[3,9,9,9,2,2,16]{6,5,4,0,3,2,1:T(2,128)} %copy.31) | data formatting | bytes 1119744 | tf_op jit(solution)/shard_map/reshape | solution.py:162
  46.7 0.8 fusion.125
  47.6 0.1 multiply_dynamic-update-slice_fusion.2
  47.7 0.0 copy-start.5
  47.7 0.1 multiply_dynamic-update-slice_fusion.1
  47.8 0.1 multiply_dynamic-update-slice_fusion
  47.9 0.6 copy-done.5
  48.5 2.9 %fusion.158 = f32[6,24,24,32]{3,2,1,0:T(8,128)S(1)} fusion(f32[6,24,24,136]{3,2,1,0:T(8,128)S(1)} %multiply_dynamic-update-slice_fusion, f32[32,136,1,1]{1,0,3,2:T(8,128)S(1)} %copy-done.5), kind=kOutput, calls=%fused_computation.409 | convolution fusion | flops 180486144 | bytes 2339840 | tf_op jit(solution)/shard_map/cxyz,kz->cxyk/dot_general | solution.py:132
  51.4 1.0 convolution_bitcast_fusion.2
  52.5 0.3 convolution_bitcast_fusion.3
  52.8 0.2 copy.28
  52.9 2.0 %slice_reduce_fusion = (f32[2,2,16]{2,1,0:T(2,128)S(1)}, f32[2,2,16]{2,1,0:T(2,128)S(1)}, f32[2,2,16]{2,1,0:T(2,128)S(1)}, f32[2,2,16]{2,1,0:T(2,128)S(1)}, f32[...) fusion(f32[6,2,2,2,2,16,2]{0,6,5,4,3,2,1:T(2,128)S(1)} %bitcast.898), kind=kLoop, calls=%fused_computation.34 | loop fusion | bytes 6144 | tf_op jit(solution)/shard_map/slice | solution.py:97
  55.0 0.1 squeeze.35
  55.1 0.1 squeeze.34
  55.1 0.1 squeeze.33
  55.2 0.1 squeeze.32
  55.3 0.1 squeeze.31
  55.4 0.1 squeeze.30
  55.5 0.1 squeeze.29
  55.6 0.1 squeeze.28
  55.6 0.1 squeeze.27
  55.7 0.1 squeeze.26
  55.8 0.1 squeeze.25
  55.9 0.1 squeeze.24
  56.4 0.3 stack.8
  56.7 0.3 concatenate.21
  57.0 0.2 fusion.159
  57.3 24.5 %psum.14 = f32[102,102]{1,0:T(8,128)S(1)} all-reduce(f32[102,102]{1,0:T(8,128)S(1)} %fusion.159), channel_id=1, replica_groups=mesh['gx'=4,'gy'=4,'gz'=2] {'gy','gz'}, use_global_device_ids=true, to_apply=%region_0.0 | all-reduce | flops 10404 | bytes 83232 | tf_op jit(solution)/shard_map/psum | solution.py:174
  81.7 19.6 %psum.15 = f32[102,102]{1,0:T(8,128)S(1)} all-reduce(f32[102,102]{1,0:T(8,128)S(1)} %psum.14), channel_id=1, replica_groups=mesh['gx'=4,'gy'=4,'gz'=2] {'gx'}, use_global_device_ids=true, to_apply=%region_1.0 | all-reduce | flops 10404 | bytes 83232 | tf_op jit(solution)/shard_map/psum | solution.py:174
  101.4 1.7 %gather_fusion = f32[102]{0:T(128)S(1)} fusion(f32[102,102]{1,0:T(8,128)S(1)} %psum.15, s32[102]{0:T(128)S(1)} %or_bitcast_fusion), kind=kCustom, calls=%fused_computation | custom fusion | bytes 1632 | tf_op jit(solution)/shard_map/jit(diagonal)/cond/branch_0_fun/gather | solution.py:108
  103.1 0.1 slice.404
  103.2 0.1 fusion.5
  103.3 0.1 copy.32
  103.4 0.1 fusion.8
  103.5 8.8 %cholesky.16 = f32[96,96]{1,0:T(8,128)S(1)} custom-call(f32[96,96]{1,0:T(8,128)S(1)} %fusion.8), custom_call_target="Cholesky" | custom-call | tf_op jit(solution)/shard_map/jit(cholesky)/cholesky | solution.py:114
  112.3 0.6 compare_reduce_fusion
  112.9 0.7 fusion.3
  113.6 7.4 %custom-call.10 = f32[1,96,96]{1,2,0:T(8,128)S(1)} custom-call(f32[1,96,96]{2,1,0:T(8,128)S(1)} %fusion.3), custom_call_target="InvertDiagBlocksLowerTriangular" | custom-call | tf_op jit(solution)/shard_map/jit(_cho_solve)/triangular_solve | solution.py:115
  120.9 0.3 fusion.4
  121.2 0.2 convolution_divide_fusion
  121.4 0.8 fusion.1
  (47 shorter events, 0.6 us)
Async XLA Ops:
  1.7 16.9 %copy-start.8 = (f32[144,136,1,1]{0,1,3,2:T(8,128)S(1)}, f32[144,136,1,1]{0,1,3,2:T(8,128)}, u32[]{:S(2)}) copy-start(f32[144,136,1,1]{0,1,3,2:T(8,128)} %constant.98) | copy-start | bytes 235012
  1.7 7.3 %collective-permute-start = (bf16[3,4,16,128]{3,2,1,0:T(8,128)(2,1)S(1)}, bf16[3,4,16,128]{3,2,1,0:T(8,128)(2,1)S(1)}, u32[]{:S(2)}, u32[]{:S(2)}) collective-permute-start(bf16[3,4,16,128]{3,2,1,0:T(8,128)(2,1)S(1)} %get-tuple-element.102), channel_id=1, source_target_pairs={{0,8},{8,16},{16,24},{24,0},{1,9},{9,17},{17,25},{25,1},{2,10},{10... | collective-permute-start | bytes 147464 | tf_op jit(solution)/shard_map/ppermute | solution.py:18
  4.8 4.6 %collective-permute-start.1 = (bf16[3,4,16,128]{3,2,1,0:T(8,128)(2,1)S(1)}, bf16[3,4,16,128]{3,2,1,0:T(8,128)(2,1)S(1)}, u32[]{:S(2)}, u32[]{:S(2)}) collective-permute-start(bf16[3,4,16,128]{3,2,1,0:T(8,128)(2,1)S(1)} %get-tuple-element.103), channel_id=1, source_target_pairs={{8,0},{16,8},{24,16},{0,24},{9,1},{17,9},{25,17},{1,25},{10,2},{18... | collective-permute-start | bytes 147464 | tf_op jit(solution)/shard_map/ppermute | solution.py:21
  9.4 10.5 %copy-start.2 = (bf16[3,4,16,128]{3,2,1,0:T(8,128)(2,1)}, bf16[3,4,16,128]{3,2,1,0:T(8,128)(2,1)S(1)}, u32[]{:S(2)}) copy-start(bf16[3,4,16,128]{3,2,1,0:T(8,128)(2,1)S(1)} %collective-permute-done.1) | copy-start | bytes 147460
  9.5 5.3 %collective-permute-start.2 = (bf16[3,24,4,128]{3,2,1,0:T(4,128)(2,1)S(1)}, bf16[3,24,4,128]{3,2,1,0:T(4,128)(2,1)S(1)}, u32[]{:S(2)}, u32[]{:S(2)}) collective-permute-start(bf16[3,24,4,128]{3,2,1,0:T(4,128)(2,1)S(1)} %get-tuple-element.100), channel_id=1, source_target_pairs={{0,2},{2,4},{4,6},{6,0},{1,3},{3,5},{5,7},{7,1},{8,10},{10,12},{12... | collective-permute-start | bytes 221192 | tf_op jit(solution)/shard_map/ppermute | solution.py:18
  11.0 4.6 %collective-permute-start.3 = (bf16[3,24,4,128]{3,2,1,0:T(4,128)(2,1)S(1)}, bf16[3,24,4,128]{3,2,1,0:T(4,128)(2,1)S(1)}, u32[]{:S(2)}, u32[]{:S(2)}) collective-permute-start(bf16[3,24,4,128]{3,2,1,0:T(4,128)(2,1)S(1)} %get-tuple-element.101), channel_id=1, source_target_pairs={{2,0},{4,2},{6,4},{0,6},{3,1},{5,3},{7,5},{1,7},{10,8},{12,10},{14... | collective-permute-start | bytes 221192 | tf_op jit(solution)/shard_map/ppermute | solution.py:21
  16.1 1.9 %collective-permute-start.4 = (bf16[3,24,24,4]{3,2,1,0:T(8,128)(2,1)S(1)}, bf16[3,24,24,4]{3,2,1,0:T(8,128)(2,1)S(1)}, u32[]{:S(2)}, u32[]{:S(2)}) collective-permute-start(bf16[3,24,24,4]{3,2,1,0:T(8,128)(2,1)S(1)} %get-tuple-element.98), channel_id=1, source_target_pairs={{0,1},{1,0},{2,3},{3,2},{4,5},{5,4},{6,7},{7,6},{8,9},{9,8},{10,11... | collective-permute-start | bytes 41480 | tf_op jit(solution)/shard_map/ppermute | solution.py:18
  16.2 2.4 %collective-permute-start.5 = (bf16[3,24,24,4]{3,2,1,0:T(8,128)(2,1)S(1)}, bf16[3,24,24,4]{3,2,1,0:T(8,128)(2,1)S(1)}, u32[]{:S(2)}, u32[]{:S(2)}) collective-permute-start(bf16[3,24,24,4]{3,2,1,0:T(8,128)(2,1)S(1)} %get-tuple-element.99), channel_id=1, source_target_pairs={{1,0},{0,1},{3,2},{2,3},{5,4},{4,5},{7,6},{6,7},{9,8},{8,9},{11,10... | collective-permute-start | bytes 41480 | tf_op jit(solution)/shard_map/ppermute | solution.py:21
  16.7 3.3 %copy-start.4 = (f32[18,24,1,1]{1,0,3,2:T(8,128)S(1)}, f32[18,24,1,1]{1,0,3,2:T(8,128)}, u32[]{:S(2)}) copy-start(f32[18,24,1,1]{1,0,3,2:T(8,128)} %constant.99) | copy-start | bytes 5188
  18.6 1.3 %copy-start = (bf16[3,24,24,4]{3,2,1,0:T(8,128)(2,1)}, bf16[3,24,24,4]{3,2,1,0:T(8,128)(2,1)S(1)}, u32[]{:S(2)}) copy-start(bf16[3,24,24,4]{3,2,1,0:T(8,128)(2,1)S(1)} %collective-permute-done.5) | copy-start | bytes 41476
  40.8 5.9 %copy-start.1 = (bf16[3,24,24,4]{3,2,1,0:T(8,128)(2,1)S(1)}, bf16[3,24,24,4]{3,2,1,0:T(8,128)(2,1)}, u32[]{:S(2)}) copy-start(bf16[3,24,24,4]{3,2,1,0:T(8,128)(2,1)} %copy-done) | copy-start | bytes 41476
  40.8 5.9 %copy-start.3 = (bf16[3,4,16,128]{3,2,1,0:T(8,128)(2,1)S(1)}, bf16[3,4,16,128]{3,2,1,0:T(8,128)(2,1)}, u32[]{:S(2)}) copy-start(bf16[3,4,16,128]{3,2,1,0:T(8,128)(2,1)} %copy-done.2) | copy-start | bytes 147460
  47.7 0.8 copy-start.5
  48.5 2.9 %copy-start.6 = (f32[4,24,1,1]{1,0,3,2:T(4,128)S(1)}, f32[4,24,1,1]{1,0,3,2:T(4,128)}, u32[]{:S(2)}) copy-start(f32[4,24,1,1]{1,0,3,2:T(4,128)} %constant.97) | copy-start | bytes 1156
  121.4 0.8 copy-start.7
